TPU v7x, 32 devices: a whole 2x2x4 slice. The times are simulated.
32 devices in a mesh: space: 8 (over y, x, core), sample: 4 (over z).
Axes of the slice: x: 2, y: 2, z: 4, core: 2. Of those that a mesh axis runs over, the one named last changes fastest.
Arguments:
- volume: bfloat16 [4, 16, 32, 64, 128], P('sample', 'space'), may hold values from -6 to 6
- upstream: bfloat16 [4, 16, 32, 64, 128], P('sample', 'space'), may hold values from -6 to 6
- weight: bfloat16 [3456, 128], replicated, may hold values from -0.109375 to 0.109375
- first_moment: float32 [3456, 128], P('sample'), may hold values from -640 to 640
- second_moment: float32 [3456, 128], P('sample'), may hold values from 262.144 to 2621.44
Outputs:
- grad_volume: bfloat16 [4, 16, 32, 64, 128], P('sample', 'space')
- direction: float32 [3456, 128], P('sample')
All inputs are finite; a program needn't handle non-finite values.
Results may differ from a plain program's by a relative error of at most 0.0039.
Values may be sent and summed in bfloat16 or wider, within the bound.
A program may use at most 64 MiB of HBM per device.

v0:
```python
import functools

import jax
import jax.numpy as jnp
from jax import lax
from jax.experimental import pallas as pl
from jax.experimental.pallas import tpu as pltpu
from jax.sharding import PartitionSpec as P

ADAM_STEP = 10

beta_one = 0.9
beta_two = 0.999
eps_adam = 1e-08

BF = jnp.bfloat16
F32 = jnp.float32
MESH = pl.DeviceIdType.MESH
CHUNKS = 4


def dot(a, b):
    return jnp.dot(a, b, preferred_element_type=F32)


def kernel(
    S, Z, h, q, e,
    vol, up, w, m_ref, v_ref,
    out, dirn,
    x3, g3, vt, wf, acc, gs, vh, gh, wg,
    s1, r1, a1, s2, r2, a2, s3, r3, a3, sx, rx, zs, zr, gsend, gbuf,
    vsend, vrecv, hsend, hrecv, st_send, st_recv, z_send, z_recv, g_send, g_recv,
):
    planes, ny, nx, ch = vol.shape
    three = 3 * ch
    nine = 3 * three
    step = ny // CHUNKS
    cells = ny * nx
    me = lax.axis_index("space")
    mz = lax.axis_index("sample")
    core = me % 2
    bx = (me // 2) % 2
    by = (me // 4) % 2
    group = me % 8
    base = me - group
    nxt = (me + 1) % S
    prv = (me + S - 1) % S
    extra = [b for b in (8, 16, 32, 64, 128) if b < S]

    def flip(bit):
        return me + bit - 2 * bit * ((me // bit) % 2)

    barrier = pltpu.get_barrier_semaphore()
    greet = [{"space": nxt}, {"space": prv}]
    greet += [{"space": base + (group + k) % 8} for k in range(1, 8)]
    greet += [{"space": flip(b)} for b in extra]
    greet += [{"sample": (mz + k) % Z} for k in range(1, Z)]
    for to in greet:
        pl.semaphore_signal(barrier, inc=1, device_id=to, device_id_type=MESH)
    pl.semaphore_wait(barrier, len(greet))

    def halo(src, dst, ssem, rsem, way, c):
        rows = pl.ds(c * step, step)
        plane = planes - 1 if way == 0 else 0
        return pltpu.make_async_remote_copy(
            src_ref=src.at[plane, rows],
            dst_ref=dst.at[way, rows],
            send_sem=ssem.at[way, c],
            recv_sem=rsem.at[way, c],
            device_id={"space": nxt if way == 0 else prv},
            device_id_type=MESH,
        )

    def has(way, sending):
        if (way == 0) == sending:
            return me < S - 1
        return me > 0

    def start_halo(src, dst, ssem, rsem, c):
        for way in range(2):
            @pl.when(has(way, True))
            def _():
                halo(src, dst, ssem, rsem, way, c).start()

    def wait_halo(src, dst, ssem, rsem, way, c):
        @pl.when(has(way, False))
        def _():
            halo(src, dst, ssem, rsem, way, c).wait_recv()

    def end_halo(src, dst, ssem, rsem):
        for way in range(2):
            @pl.when(has(way, True))
            def _():
                for c in range(CHUNKS):
                    halo(src, dst, ssem, rsem, way, c).wait_send()

    for c in range(CHUNKS):
        start_halo(vol, vh, vsend, vrecv, c)

    part = 4
    pos = lax.broadcasted_iota(jnp.int32, (part * nx, ch), 0) % nx

    def put3(dst, zi, row, val):
        n = part * nx
        at = pl.ds(row + 1, part)
        before = jnp.where(pos == 0, 0.0, pltpu.roll(val, 1, 0))
        after = jnp.where(pos == nx - 1, 0.0, pltpu.roll(val, n - 1, 0))
        dst[zi, at, :, 0:ch] = before.astype(BF).reshape(part, nx, ch)
        dst[zi, at, :, ch : 2 * ch] = val.astype(BF).reshape(part, nx, ch)
        dst[zi, at, :, 2 * ch :] = after.astype(BF).reshape(part, nx, ch)

    def fill(dst, zi, src, p, first, count):
        def one(i, _):
            row = first + i * part
            put3(dst, zi, row, src[p, pl.ds(row, part)].astype(F32).reshape(part * nx, ch))
            return 0
        lax.fori_loop(0, count // part, one, 0)

    def fill_halo(dst, src, way, first, count):
        zi = 0 if way == 0 else planes + 1

        @pl.when(has(way, False))
        def _():
            fill(dst, zi, src, way, first, count)

    for buf in (x3, g3):
        for zi in range(planes + 2):
            buf[zi, 0] = jnp.zeros((nx, three), BF)
            buf[zi, ny + 1] = jnp.zeros((nx, three), BF)
        for way in range(2):
            @pl.when(jnp.logical_not(has(way, False)))
            def _():
                zi = 0 if way == 0 else planes + 1

                def clear(i, _):
                    buf[zi, i + 1] = jnp.zeros((nx, three), BF)
                    return 0
                lax.fori_loop(0, ny, clear, 0)

    def turn(zi):
        def one(j, _):
            cols = 2 * ch // nx
            t = x3[zi, pl.ds(1 + cols * j, cols)].reshape(2 * ch, three)
            vt[zi, :, pl.ds(pl.multiple_of(j * 2 * ch, 2 * ch), 2 * ch)] = t.T
            return 0
        lax.fori_loop(0, cells // (2 * ch), one, 0)

    def taps(buf, zi, y0):
        return [buf[zi, pl.ds(y0 + dy, step)].reshape(step * nx, three) for dy in range(3)]

    def inner(buf, wt, zo):
        lo = max(1, zo)
        hi = min(planes, zo + 2)

        def one(c, _):
            y0 = c * step
            lhs = jnp.concatenate(sum([taps(buf, zi, y0) for zi in range(lo, hi + 1)], []), axis=1)
            acc[zo, pl.ds(y0, step)] = dot(lhs, wt[pl.ds((lo - zo) * nine, (hi + 1 - lo) * nine)]).reshape(step, nx, ch)
            return 0
        lax.fori_loop(0, CHUNKS, one, 0)

    def outer(buf, wt, zo, y0):
        res = acc[zo, pl.ds(y0, step)].reshape(step * nx, ch)
        for zi in (0, planes + 1):
            if zo <= zi <= zo + 2:
                res += dot(jnp.concatenate(taps(buf, zi, y0), axis=1), wt[pl.ds((zi - zo) * nine, nine)])
        return res

    for p in range(planes):
        fill(x3, p + 1, vol, p, 0, ny)
    for zo in range(planes):
        inner(x3, w, zo)
    for p in range(planes):
        turn(p + 1)

    def flip_w(t, _):
        src = pl.multiple_of((26 - t) * ch, ch)
        wf[pl.ds(pl.multiple_of(t * ch, ch), ch)] = w[pl.ds(src, ch)].T
        return 0
    lax.fori_loop(0, 27, flip_w, 0)

    def arrive(buf, raw, ssem, rsem, src, c):
        for way in range(2):
            wait_halo(src, raw, ssem, rsem, way, c)
            fill_halo(buf, raw, way, c * step, step)

    for c in range(CHUNKS):
        if c == 0:
            arrive(x3, vh, vsend, vrecv, vol, 0)
        if c + 1 < CHUNKS:
            arrive(x3, vh, vsend, vrecv, vol, c + 1)
        for zo in range(planes):
            y0 = c * step
            acc[zo, pl.ds(y0, step)] = outer(x3, w, zo, y0).reshape(step, nx, ch)

            def slope(i, _):
                at = pl.ds(y0 + i * part, part)
                pre = acc[zo, at].reshape(part * nx, ch)
                u = up[zo, at].astype(F32).reshape(part * nx, ch)
                s = jax.nn.sigmoid(pre)
                g = (u * (s * (1.0 + pre * (1.0 - s)))).astype(BF)
                gs[zo, at] = g.reshape(part, nx, ch)
                put3(g3, zo + 1, y0 + i * part, g.astype(F32))
                return 0
            lax.fori_loop(0, step // part, slope, 0)
        start_halo(gs, gh, hsend, hrecv, c)

    turn(0)
    turn(planes + 1)

    def grad(dz, _):
        for zo in range(planes):
            rhs = jnp.concatenate(
                [g3[zo + 1, 2 - dy : 2 - dy + ny, :, ch : 2 * ch].reshape(cells, ch) for dy in range(3)], axis=1
            )
            res = dot(vt[dz + zo], rhs)
            for dy in range(3):
                at = pl.ds(pl.multiple_of((dz * 3 + dy) * three, three), three)
                piece = res[:, dy * ch : (dy + 1) * ch]
                if zo == 0:
                    wg[at] = piece
                else:
                    wg[at] += piece
        return 0
    lax.fori_loop(0, 3, grad, 0)

    def swap(i, src, dst, to):
        return pltpu.make_async_remote_copy(
            src_ref=src, dst_ref=dst, send_sem=st_send.at[i], recv_sem=st_recv.at[i],
            device_id={"space": to}, device_id_type=MESH,
        )

    own = 2 * h

    def cut(ref, z, where, size, unit):
        return ref[z, pl.ds(pl.multiple_of(where, unit), size)]

    second = bx + core * (by - bx)
    third = by + core * (bx - by)
    to_second = flip(2) + core * (flip(4) - flip(2))
    to_third = flip(4) + core * (flip(2) - flip(4))

    for z in range(Z):
        s1[z] = wg[pl.ds(pl.multiple_of(z * own + h * (1 - core), 16), h)].astype(BF)
    first_swap = swap(0, s1, r1, flip(1))
    first_swap.start()
    inner(g3, wf, 0)
    first_swap.wait()
    for z in range(Z):
        a1[z] = wg[pl.ds(pl.multiple_of(z * own + h * core, 16), h)] + r1[z].astype(F32)
        s2[z] = cut(a1, z, (h - q) * (1 - second), q, 16).astype(BF)
    second_swap = swap(1, s2, r2, to_second)
    second_swap.start()
    for zo in range(1, planes):
        inner(g3, wf, zo)
    second_swap.wait()
    for z in range(Z):
        a2[z] = cut(a1, z, (h - q) * second, q, 16) + r2[z].astype(F32)
        s3[z] = cut(a2, z, e * (1 - third), e, 16).astype(BF)
    third_swap = swap(2, s3, r3, to_third)
    third_swap.start()

    def finish(zo):
        def one(c, _):
            y0 = c * step
            res = outer(g3, wf, zo, y0) + up[zo, pl.ds(y0, step)].astype(F32).reshape(step * nx, ch)
            out[zo, pl.ds(y0, step)] = res.astype(BF).reshape(step, nx, ch)
            return 0
        lax.fori_loop(0, CHUNKS, one, 0)

    third_swap.wait()
    for z in range(Z):
        a3[z] = cut(a2, z, e * third, e, 16) + r3[z].astype(F32)
    for i, bit in enumerate(extra):
        for z in range(Z):
            sx[i, z] = a3[z].astype(BF)
        more = swap(3 + i, sx.at[i], rx.at[i], flip(bit))
        more.start()
        more.wait()
        for z in range(Z):
            a3[z] = sx[i, z].astype(F32) + rx[i, z].astype(F32)

    def z_copy(k):
        return pltpu.make_async_remote_copy(
            src_ref=zs.at[(mz + k) % Z], dst_ref=zr.at[k - 1], send_sem=z_send.at[k - 1], recv_sem=z_recv.at[k - 1],
            device_id={"sample": (mz + k) % Z}, device_id_type=MESH,
        )

    for z in range(Z):
        zs[z] = a3[z].astype(BF)
    for k in range(1, Z):
        z_copy(k).start()

    for c in range(CHUNKS):
        arrive(g3, gh, hsend, hrecv, gs, c)
    finish(0)
    for k in range(1, Z):
        z_copy(k).wait()
    total = a3[mz]
    for k in range(1, Z):
        total += zr[k - 1].astype(F32)
    gsend[...] = total.astype(BF)

    def slot(g):
        c, x, y = g % 2, (g // 2) % 2, g // 4
        return 4 * c + 2 * (x + c * (y - x)) + (y + c * (x - y))

    def g_copy(k, place):
        return pltpu.make_async_remote_copy(
            src_ref=gsend, dst_ref=gbuf.at[place], send_sem=g_send.at[k - 1], recv_sem=g_recv.at[k - 1],
            device_id={"space": base + (group + k) % 8}, device_id_type=MESH,
        )

    for k in range(1, 8):
        g_copy(k, slot(group)).start()
    gbuf[slot(group)] = total.astype(BF)
    for zo in range(1, planes):
        finish(zo)
    for k in range(1, 8):
        g_copy(k, slot((group + 8 - k) % 8)).wait_recv()
    for i in range(8):
        at = pl.ds(h * (i // 4) + (h - q) * ((i // 2) % 2) + e * (i % 2), e)
        share = gbuf[i].astype(F32)
        m_new = beta_one * m_ref[at] + (1.0 - beta_one) * share
        v_new = beta_two * v_ref[at] + (1.0 - beta_two) * share * share
        dirn[at] = m_new / (1.0 - beta_one**ADAM_STEP) / (jnp.sqrt(v_new / (1.0 - beta_two**ADAM_STEP)) + eps_adam)
    for k in range(1, 8):
        g_copy(k, slot(group)).wait_send()
    end_halo(vol, vh, vsend, vrecv)
    end_halo(gs, gh, hsend, hrecv)


def body(S, Z, volume, upstream, weight, first_moment, second_moment):
    _, planes, ny, nx, ch = volume.shape
    rows = first_moment.shape[0]
    h = rows // 2
    q = -(-h // 64) * 32
    e = q // 2
    n_extra = max(1, S.bit_length() - 4)
    halo_shape = (2, ny, nx, ch)
    padded = (planes + 2, ny + 2, nx, 3 * ch)
    dma = pltpu.SemaphoreType.DMA
    vm = pltpu.VMEM
    grad_volume, direction = pl.pallas_call(
        functools.partial(kernel, S, Z, h, q, e),
        out_shape=(
            jax.ShapeDtypeStruct((planes, ny, nx, ch), BF),
            jax.ShapeDtypeStruct((rows, ch), F32),
        ),
        in_specs=[pl.BlockSpec(memory_space=pltpu.VMEM)] * 5,
        out_specs=(pl.BlockSpec(memory_space=pltpu.VMEM),) * 2,
        scratch_shapes=[
            vm(padded, BF),
            vm(padded, BF),
            vm((planes + 2, 3 * ch, ny * nx), BF),
            vm(weight.shape, BF),
            vm((planes, ny, nx, ch), F32),
            vm((planes, ny, nx, ch), BF),
            vm(halo_shape, BF),
            vm(halo_shape, BF),
            vm(weight.shape, F32),
            vm((Z, h, ch), BF),
            vm((Z, h, ch), BF),
            vm((Z, h, ch), F32),
            vm((Z, q, ch), BF),
            vm((Z, q, ch), BF),
            vm((Z, q, ch), F32),
            vm((Z, e, ch), BF),
            vm((Z, e, ch), BF),
            vm((Z, e, ch), F32),
            vm((n_extra, Z, e, ch), BF),
            vm((n_extra, Z, e, ch), BF),
            vm((Z, e, ch), BF),
            vm((Z - 1, e, ch), BF),
            vm((e, ch), BF),
            vm((8, e, ch), BF),
            dma((2, CHUNKS)),
            dma((2, CHUNKS)),
            dma((2, CHUNKS)),
            dma((2, CHUNKS)),
            dma((3 + n_extra,)),
            dma((3 + n_extra,)),
            dma((Z - 1,)),
            dma((Z - 1,)),
            dma((7,)),
            dma((7,)),
        ],
        compiler_params=pltpu.CompilerParams(
            collective_id=0, has_side_effects=True, vmem_limit_bytes=60 * 1024 * 1024
        ),
        name="block",
    )(volume[0], upstream[0], weight, first_moment, second_moment)
    return grad_volume[None], direction


def solution(mesh):
    return jax.shard_map(
        functools.partial(body, mesh.shape["space"], mesh.shape["sample"]),
        mesh=mesh,
        in_specs=(
            P("sample", "space", None, None, None),
            P("sample", "space", None, None, None),
            P(),
            P("sample", None),
            P("sample", None),
        ),
        out_specs=(P("sample", "space", None, None, None), P("sample", None)),
        check_vma=False,
    )
```

profile of v0, /device:TPU:0, one launch (start us, length us, event | category | flops | bytes accessed | tf_op | source)
XLA Modules:
  0.0 57.8 jit_solution(3775836879934569035)
XLA Ops:
  0.6 54.1 %block.1 = (bf16[2,32,64,128]{3,2,1,0:T(8,128)(2,1)}, f32[864,128]{1,0:T(8,128)}) custom-call(bf16[2,32,64,128]{3,2,1,0:T(8,128)(2,1)} %bitcast.4, bf16[2,32,64,128]{3,2,1,0:T(8,128)(2,1)} %bitcast.5, bf16[3456,128]{1,0:T(8,128)(2,1)} %w.1, f32[864,128]{1,0:T(8,128)} %m_ref.1, f32[864,128]{1,0:T(8,128)} %v_ref.1), custom_call_target="tpu_custom_call" | custom-call | tf_op jit(solution)/shard_map/block/pallas_call | solution.py:344
  54.7 0.0 copy-start
  54.7 2.3 %copy.9 = bf16[1,2,32,64,128]{4,3,2,1,0:T(8,128)(2,1)} copy(bf16[1,2,32,64,128]{4,3,2,1,0:T(8,128)(2,1)} %bitcast.3) | data formatting | bytes 2097152
  57.0 0.0 copy-done
  57.0 0.8 %copy.10 = f32[864,128]{1,0:T(8,128)} copy(f32[864,128]{1,0:T(8,128)S(1)} %copy-done) | data formatting | bytes 884736
Async XLA Ops:
  54.7 2.3 %copy-start = (f32[864,128]{1,0:T(8,128)S(1)}, f32[864,128]{1,0:T(8,128)}, u32[]{:S(2)}) copy-start(f32[864,128]{1,0:T(8,128)} %get-tuple-element.9) | copy-start | bytes 1327108
where the time goes:
time: 58 us; the launch traced here: 57.8 us
  Pallas kernels  54.1 us (93%)
  local copies, waits for them, and re-layouts  3.08 us (5%)
  between operations  0.65 us (1%)
    pallas_call x1, Pallas kernels, body(): pl.pallas_call(functools.partial(kernel, S, Z, h, q, e), out_shape=(jax.S...  54.1 us
    unnamed x4, local copies, waits for them, and re-layouts  3.08 us

commit v1 on v0

--- a/solution.py
+++ b/solution.py
@@ -25,13 +25,20 @@
 
 def kernel(
     S, Z, h, q, e,
-    vol, up, w, m_ref, v_ref,
-    out, dirn,
+    vol_in, up_in, w_in, m_in, v_in,
+    out_hbm, dirn,
+    vol, up, w, m_ref, v_ref, out,
     x3, g3, vt, wf, acc, gs, vh, gh, wg,
     s1, r1, a1, s2, r2, a2, s3, r3, a3, sx, rx, zs, zr, gsend, gbuf,
-    vsend, vrecv, hsend, hrecv, st_send, st_recv, z_send, z_recv, g_send, g_recv,
+    io_sem, vsend, vrecv, hsend, hrecv, st_send, st_recv, z_send, z_recv, g_send, g_recv,
 ):
     planes, ny, nx, ch = vol.shape
+    loads = [
+        pltpu.make_async_copy(a, b, io_sem.at[i])
+        for i, (a, b) in enumerate(((vol_in, vol), (w_in, w), (up_in, up), (m_in, m_ref), (v_in, v_ref)))
+    ]
+    for load in loads:
+        load.start()
     three = 3 * ch
     nine = 3 * three
     step = ny // CHUNKS
@@ -94,8 +101,38 @@
                 for c in range(CHUNKS):
                     halo(src, dst, ssem, rsem, way, c).wait_send()
 
+    relayed = range(CHUNKS // 2, CHUNKS) if S == 8 else ()
+    senders, relays = (S // 2 - 1, S // 2), (S - 1, 0)
+
+    def hop(way, c):
+        rows = pl.ds(c * step, step)
+        return pltpu.make_async_remote_copy(
+            src_ref=vol_in.at[planes - 1 if way == 0 else 0, rows], dst_ref=vh.at[1 - way, rows],
+            send_sem=vsend.at[way, c], recv_sem=vrecv.at[1 - way, c],
+            device_id={"space": relays[way]}, device_id_type=MESH,
+        )
+
+    def pass_on(way, c):
+        rows = pl.ds(c * step, step)
+        return pltpu.make_async_remote_copy(
+            src_ref=vh.at[1 - way, rows], dst_ref=vh.at[way, rows],
+            send_sem=vsend.at[way, c], recv_sem=vrecv.at[way, c],
+            device_id={"space": senders[1 - way]}, device_id_type=MESH,
+        )
+
+    for c in relayed:
+        for way in range(2):
+            @pl.when(me == senders[way])
+            def _():
+                hop(way, c).start()
     for c in range(CHUNKS):
-        start_halo(vol, vh, vsend, vrecv, c)
+        if c not in relayed:
+            start_halo(vol_in, vh, vsend, vrecv, c)
+            continue
+        for way in range(2):
+            @pl.when(jnp.logical_and(has(way, True), me != senders[way]))
+            def _():
+                halo(vol_in, vh, vsend, vrecv, way, c).start()
 
     part = 4
     pos = lax.broadcasted_iota(jnp.int32, (part * nx, ch), 0) % nx
@@ -148,28 +185,48 @@
     def taps(buf, zi, y0):
         return [buf[zi, pl.ds(y0 + dy, step)].reshape(step * nx, three) for dy in range(3)]
 
-    def inner(buf, wt, zo):
-        lo = max(1, zo)
-        hi = min(planes, zo + 2)
+    half = step // 2
+
+    def inner(buf, wt):
+        rhs = jnp.concatenate([wt[nine : 3 * nine], wt[0 : 2 * nine]], axis=1)
 
         def one(c, _):
             y0 = c * step
-            lhs = jnp.concatenate(sum([taps(buf, zi, y0) for zi in range(lo, hi + 1)], []), axis=1)
-            acc[zo, pl.ds(y0, step)] = dot(lhs, wt[pl.ds((lo - zo) * nine, (hi + 1 - lo) * nine)]).reshape(step, nx, ch)
+            lhs = jnp.concatenate(taps(buf, 1, y0) + taps(buf, 2, y0), axis=1)
+            res = dot(lhs, rhs)
+            at = pl.ds(c * half, half)
+            for zo in range(2):
+                acc[zo, at] = res[:, zo * ch : (zo + 1) * ch].reshape(half, 2, nx, ch)
             return 0
         lax.fori_loop(0, CHUNKS, one, 0)
 
-    def outer(buf, wt, zo, y0):
-        res = acc[zo, pl.ds(y0, step)].reshape(step * nx, ch)
-        for zi in (0, planes + 1):
-            if zo <= zi <= zo + 2:
-                res += dot(jnp.concatenate(taps(buf, zi, y0), axis=1), wt[pl.ds((zi - zo) * nine, nine)])
-        return res
-
+    def outer(buf, wt, zo, c):
+        zi = 3 * zo
+        own_rows = wt[2 * zo * nine : (2 * zo + 1) * nine]
+        gap = jnp.zeros((three, ch), BF)
+        rhs = jnp.concatenate(
+            [jnp.concatenate([own_rows, gap], axis=0), jnp.concatenate([gap, own_rows], axis=0)], axis=1
+        )
+        rows = buf[zi, pl.ds(c * step, step + 2)].reshape(half + 1, 2, nx, three)
+        lhs = jnp.concatenate(
+            [rows[d // 2 : d // 2 + half, d % 2].reshape(half * nx, three) for d in range(4)], axis=1
+        )
+        res = dot(lhs, rhs)
+        at = pl.ds(c * half, half)
+        for odd in range(2):
+            acc[zo, at, odd] += res[:, odd * ch : (odd + 1) * ch].reshape(half, nx, ch)
+
+    loads[0].wait()
     for p in range(planes):
         fill(x3, p + 1, vol, p, 0, ny)
-    for zo in range(planes):
-        inner(x3, w, zo)
+    loads[1].wait()
+    inner(x3, w)
+    for c in relayed:
+        for way in range(2):
+            @pl.when(me == relays[way])
+            def _():
+                hop(way, c).wait_recv()
+                pass_on(way, c).start()
     for p in range(planes):
         turn(p + 1)
 
@@ -178,6 +235,7 @@
         wf[pl.ds(pl.multiple_of(t * ch, ch), ch)] = w[pl.ds(src, ch)].T
         return 0
     lax.fori_loop(0, 27, flip_w, 0)
+    loads[2].wait()
 
     def arrive(buf, raw, ssem, rsem, src, c):
         for way in range(2):
@@ -186,18 +244,18 @@
 
     for c in range(CHUNKS):
         if c == 0:
-            arrive(x3, vh, vsend, vrecv, vol, 0)
+            arrive(x3, vh, vsend, vrecv, vol_in, 0)
         if c + 1 < CHUNKS:
-            arrive(x3, vh, vsend, vrecv, vol, c + 1)
+            arrive(x3, vh, vsend, vrecv, vol_in, c + 1)
         for zo in range(planes):
             y0 = c * step
-            acc[zo, pl.ds(y0, step)] = outer(x3, w, zo, y0).reshape(step, nx, ch)
+            outer(x3, w, zo, c)
 
             def slope(i, _):
                 at = pl.ds(y0 + i * part, part)
-                pre = acc[zo, at].reshape(part * nx, ch)
+                pre = acc[zo, pl.ds(y0 // 2 + i * (part // 2), part // 2)].reshape(part * nx, ch)
                 u = up[zo, at].astype(F32).reshape(part * nx, ch)
-                s = jax.nn.sigmoid(pre)
+                s = 0.5 + 0.5 * jnp.tanh(0.5 * pre)
                 g = (u * (s * (1.0 + pre * (1.0 - s)))).astype(BF)
                 gs[zo, at] = g.reshape(part, nx, ch)
                 put3(g3, zo + 1, y0 + i * part, g.astype(F32))
@@ -240,19 +298,32 @@
     to_second = flip(2) + core * (flip(4) - flip(2))
     to_third = flip(4) + core * (flip(2) - flip(4))
 
+    def store(zo):
+        return pltpu.make_async_copy(out.at[zo], out_hbm.at[zo], io_sem.at[5 + zo])
+
+    def finish(zo):
+        for c in range(CHUNKS):
+            outer(g3, wf, zo, c)
+
+            def one(i, _):
+                row = c * step + i * part
+                res = acc[zo, pl.ds(c * half + i * (part // 2), part // 2)].reshape(part, nx, ch)
+                out[zo, pl.ds(row, part)] = (res + up[zo, pl.ds(row, part)].astype(F32)).astype(BF)
+                return 0
+            lax.fori_loop(0, step // part, one, 0)
+        store(zo).start()
+
     for z in range(Z):
         s1[z] = wg[pl.ds(pl.multiple_of(z * own + h * (1 - core), 16), h)].astype(BF)
     first_swap = swap(0, s1, r1, flip(1))
     first_swap.start()
-    inner(g3, wf, 0)
     first_swap.wait()
     for z in range(Z):
         a1[z] = wg[pl.ds(pl.multiple_of(z * own + h * core, 16), h)] + r1[z].astype(F32)
         s2[z] = cut(a1, z, (h - q) * (1 - second), q, 16).astype(BF)
     second_swap = swap(1, s2, r2, to_second)
     second_swap.start()
-    for zo in range(1, planes):
-        inner(g3, wf, zo)
+    inner(g3, wf)
     second_swap.wait()
     for z in range(Z):
         a2[z] = cut(a1, z, (h - q) * second, q, 16) + r2[z].astype(F32)
@@ -260,14 +331,8 @@
     third_swap = swap(2, s3, r3, to_third)
     third_swap.start()
 
-    def finish(zo):
-        def one(c, _):
-            y0 = c * step
-            res = outer(g3, wf, zo, y0) + up[zo, pl.ds(y0, step)].astype(F32).reshape(step * nx, ch)
-            out[zo, pl.ds(y0, step)] = res.astype(BF).reshape(step, nx, ch)
-            return 0
-        lax.fori_loop(0, CHUNKS, one, 0)
-
+    for c in range(CHUNKS):
+        arrive(g3, gh, hsend, hrecv, gs, c)
     third_swap.wait()
     for z in range(Z):
         a3[z] = cut(a2, z, e * third, e, 16) + r3[z].astype(F32)
@@ -291,8 +356,6 @@
     for k in range(1, Z):
         z_copy(k).start()
 
-    for c in range(CHUNKS):
-        arrive(g3, gh, hsend, hrecv, gs, c)
     finish(0)
     for k in range(1, Z):
         z_copy(k).wait()
@@ -314,10 +377,11 @@
     for k in range(1, 8):
         g_copy(k, slot(group)).start()
     gbuf[slot(group)] = total.astype(BF)
-    for zo in range(1, planes):
-        finish(zo)
+    finish(1)
     for k in range(1, 8):
         g_copy(k, slot((group + 8 - k) % 8)).wait_recv()
+    loads[3].wait()
+    loads[4].wait()
     for i in range(8):
         at = pl.ds(h * (i // 4) + (h - q) * ((i // 2) % 2) + e * (i % 2), e)
         share = gbuf[i].astype(F32)
@@ -326,13 +390,21 @@
         dirn[at] = m_new / (1.0 - beta_one**ADAM_STEP) / (jnp.sqrt(v_new / (1.0 - beta_two**ADAM_STEP)) + eps_adam)
     for k in range(1, 8):
         g_copy(k, slot(group)).wait_send()
-    end_halo(vol, vh, vsend, vrecv)
+    for c in relayed:
+        for way in range(2):
+            @pl.when(me == relays[way])
+            def _():
+                pass_on(way, c).wait_send()
+    for zo in range(planes):
+        store(zo).wait()
+    end_halo(vol_in, vh, vsend, vrecv)
     end_halo(gs, gh, hsend, hrecv)
 
 
 def body(S, Z, volume, upstream, weight, first_moment, second_moment):
     _, planes, ny, nx, ch = volume.shape
     rows = first_moment.shape[0]
+    assert planes == 2
     h = rows // 2
     q = -(-h // 64) * 32
     e = q // 2
@@ -347,14 +419,20 @@
             jax.ShapeDtypeStruct((planes, ny, nx, ch), BF),
             jax.ShapeDtypeStruct((rows, ch), F32),
         ),
-        in_specs=[pl.BlockSpec(memory_space=pltpu.VMEM)] * 5,
-        out_specs=(pl.BlockSpec(memory_space=pltpu.VMEM),) * 2,
+        in_specs=[pl.BlockSpec(memory_space=pl.ANY)] * 5,
+        out_specs=(pl.BlockSpec(memory_space=pl.ANY), pl.BlockSpec(memory_space=pltpu.VMEM)),
         scratch_shapes=[
+            vm((planes, ny, nx, ch), BF),
+            vm((planes, ny, nx, ch), BF),
+            vm(weight.shape, BF),
+            vm((rows, ch), F32),
+            vm((rows, ch), F32),
+            vm((planes, ny, nx, ch), BF),
             vm(padded, BF),
             vm(padded, BF),
             vm((planes + 2, 3 * ch, ny * nx), BF),
             vm(weight.shape, BF),
-            vm((planes, ny, nx, ch), F32),
+            vm((planes, ny // 2, 2, nx, ch), F32),
             vm((planes, ny, nx, ch), BF),
             vm(halo_shape, BF),
             vm(halo_shape, BF),
@@ -374,6 +452,7 @@
             vm((Z - 1, e, ch), BF),
             vm((e, ch), BF),
             vm((8, e, ch), BF),
+            dma((5 + planes,)),
             dma((2, CHUNKS)),
             dma((2, CHUNKS)),
             dma((2, CHUNKS)),

time: 58 us -> 50.7 us (0.87)
  Pallas kernels: 54.1 us -> 46.8 us
    pallas_call x1, Pallas kernels: 54.1 us -> 46.8 us  [body(): pl.pallas_call(functools.partial(kernel, S, Z, h, q, e), out_shape=(jax.S...]
where the time goes in v1:
time: 50.7 us; the launch traced here: 50.6 us
  Pallas kernels  46.8 us (92%)
  local copies, waits for them, and re-layouts  3.08 us (6%)
  between operations  0.65 us (1%)
    pallas_call x1, Pallas kernels, body(): pl.pallas_call(functools.partial(kernel, S, Z, h, q, e), out_shape=(jax.S...  46.8 us
    unnamed x4, local copies, waits for them, and re-layouts  3.08 us

profile of v1, /device:TPU:0, one launch (start us, length us, event | category | flops | bytes accessed | tf_op | source)
XLA Modules:
  0.0 50.6 jit_solution(16025889098182384248)
XLA Ops:
  0.6 46.8 %block.1 = (bf16[2,32,64,128]{3,2,1,0:T(8,128)(2,1)}, f32[864,128]{1,0:T(8,128)}) custom-call(bf16[2,32,64,128]{3,2,1,0:T(8,128)(2,1)} %bitcast.4, bf16[2,32,64,128]{3,2,1,0:T(8,128)(2,1)} %bitcast.5, bf16[3456,128]{1,0:T(8,128)(2,1)} %w_in.1, f32[864,128]{1,0:T(8,128)} %m_in.1, f32[864,128]{1,0:T(8,128)} %v_in.1), custom_call_target="tpu_custom_call" | custom-call | tf_op jit(solution)/shard_map/block/pallas_call | solution.py:416
  47.5 0.0 copy-start
  47.5 2.3 %copy.9 = bf16[1,2,32,64,128]{4,3,2,1,0:T(8,128)(2,1)} copy(bf16[1,2,32,64,128]{4,3,2,1,0:T(8,128)(2,1)} %bitcast.3) | data formatting | bytes 2097152
  49.8 0.0 copy-done
  49.8 0.8 %copy.10 = f32[864,128]{1,0:T(8,128)} copy(f32[864,128]{1,0:T(8,128)S(1)} %copy-done) | data formatting | bytes 884736
Async XLA Ops:
  47.5 2.3 %copy-start = (f32[864,128]{1,0:T(8,128)S(1)}, f32[864,128]{1,0:T(8,128)}, u32[]{:S(2)}) copy-start(f32[864,128]{1,0:T(8,128)} %get-tuple-element.9) | copy-start | bytes 1327108

commit v2 on v1

--- a/solution.py
+++ b/solution.py
@@ -151,7 +151,7 @@
             row = first + i * part
             put3(dst, zi, row, src[p, pl.ds(row, part)].astype(F32).reshape(part * nx, ch))
             return 0
-        lax.fori_loop(0, count // part, one, 0)
+        lax.fori_loop(0, count // part, one, 0, unroll=2)
 
     def fill_halo(dst, src, way, first, count):
         zi = 0 if way == 0 else planes + 1
@@ -180,7 +180,7 @@
             t = x3[zi, pl.ds(1 + cols * j, cols)].reshape(2 * ch, three)
             vt[zi, :, pl.ds(pl.multiple_of(j * 2 * ch, 2 * ch), 2 * ch)] = t.T
             return 0
-        lax.fori_loop(0, cells // (2 * ch), one, 0)
+        lax.fori_loop(0, cells // (2 * ch), one, 0, unroll=4)
 
     def taps(buf, zi, y0):
         return [buf[zi, pl.ds(y0 + dy, step)].reshape(step * nx, three) for dy in range(3)]
@@ -234,7 +234,7 @@
         src = pl.multiple_of((26 - t) * ch, ch)
         wf[pl.ds(pl.multiple_of(t * ch, ch), ch)] = w[pl.ds(src, ch)].T
         return 0
-    lax.fori_loop(0, 27, flip_w, 0)
+    lax.fori_loop(0, 27, flip_w, 0, unroll=3)
     loads[2].wait()
 
     def arrive(buf, raw, ssem, rsem, src, c):
@@ -260,27 +260,30 @@
                 gs[zo, at] = g.reshape(part, nx, ch)
                 put3(g3, zo + 1, y0 + i * part, g.astype(F32))
                 return 0
-            lax.fori_loop(0, step // part, slope, 0)
+            lax.fori_loop(0, step // part, slope, 0, unroll=True)
         start_halo(gs, gh, hsend, hrecv, c)
 
+    def g_rows(zo):
+        return [g3[zo + 1, 2 - dy : 2 - dy + ny, :, ch : 2 * ch].reshape(cells, ch) for dy in range(3)]
+
+    def put_grad(dz, res, at0, add):
+        for dy in range(3):
+            at = pl.ds((dz * 3 + dy) * three, three)
+            piece = res[:, at0 + dy * ch : at0 + (dy + 1) * ch]
+            if add:
+                wg[at] += piece
+            else:
+                wg[at] = piece
+
+    both = jnp.concatenate(g_rows(0) + g_rows(1), axis=1)
+    for zi in (1, 2):
+        res = dot(vt[zi], both)
+        put_grad(zi, res, 0, False)
+        put_grad(zi - 1, res, three, zi == 2)
     turn(0)
+    put_grad(0, dot(vt[0], jnp.concatenate(g_rows(0), axis=1)), 0, True)
     turn(planes + 1)
-
-    def grad(dz, _):
-        for zo in range(planes):
-            rhs = jnp.concatenate(
-                [g3[zo + 1, 2 - dy : 2 - dy + ny, :, ch : 2 * ch].reshape(cells, ch) for dy in range(3)], axis=1
-            )
-            res = dot(vt[dz + zo], rhs)
-            for dy in range(3):
-                at = pl.ds(pl.multiple_of((dz * 3 + dy) * three, three), three)
-                piece = res[:, dy * ch : (dy + 1) * ch]
-                if zo == 0:
-                    wg[at] = piece
-                else:
-                    wg[at] += piece
-        return 0
-    lax.fori_loop(0, 3, grad, 0)
+    put_grad(2, dot(vt[3], jnp.concatenate(g_rows(1), axis=1)), 0, True)
 
     def swap(i, src, dst, to):
         return pltpu.make_async_remote_copy(

time: 50.7 us -> 47.4 us (0.935)
  Pallas kernels: 46.8 us -> 43.5 us
    pallas_call x1, Pallas kernels: 46.8 us -> 43.5 us  [body(): pl.pallas_call(functools.partial(kernel, S, Z, h, q, e), out_shape=(jax.S...]
where the time goes in v2:
time: 47.4 us; the launch traced here: 47.3 us
  Pallas kernels  43.5 us (92%)
  local copies, waits for them, and re-layouts  3.08 us (6%)
  between operations  0.65 us (1%)
    pallas_call x1, Pallas kernels, body(): pl.pallas_call(functools.partial(kernel, S, Z, h, q, e), out_shape=(jax.S...  43.5 us
    unnamed x4, local copies, waits for them, and re-layouts  3.08 us

profile of v2, /device:TPU:0, one launch (start us, length us, event | category | flops | bytes accessed | tf_op | source)
XLA Modules:
  0.0 47.3 jit_solution(10850145556149987466)
XLA Ops:
  0.6 43.5 %block.1 = (bf16[2,32,64,128]{3,2,1,0:T(8,128)(2,1)}, f32[864,128]{1,0:T(8,128)}) custom-call(bf16[2,32,64,128]{3,2,1,0:T(8,128)(2,1)} %bitcast.4, bf16[2,32,64,128]{3,2,1,0:T(8,128)(2,1)} %bitcast.5, bf16[3456,128]{1,0:T(8,128)(2,1)} %w_in.1, f32[864,128]{1,0:T(8,128)} %m_in.1, f32[864,128]{1,0:T(8,128)} %v_in.1), custom_call_target="tpu_custom_call" | custom-call | tf_op jit(solution)/shard_map/block/pallas_call | solution.py:419
  44.2 0.0 copy-start
  44.2 2.3 %copy.9 = bf16[1,2,32,64,128]{4,3,2,1,0:T(8,128)(2,1)} copy(bf16[1,2,32,64,128]{4,3,2,1,0:T(8,128)(2,1)} %bitcast.3) | data formatting | bytes 2097152
  46.5 0.0 copy-done
  46.5 0.8 %copy.10 = f32[864,128]{1,0:T(8,128)} copy(f32[864,128]{1,0:T(8,128)S(1)} %copy-done) | data formatting | bytes 884736
Async XLA Ops:
  44.2 2.3 %copy-start = (f32[864,128]{1,0:T(8,128)S(1)}, f32[864,128]{1,0:T(8,128)}, u32[]{:S(2)}) copy-start(f32[864,128]{1,0:T(8,128)} %get-tuple-element.9) | copy-start | bytes 1327108
